TPU v7x, 32 devices: a whole 2x2x4 slice. The times are simulated.
32 devices in a mesh: groups: 2 (over x), pop: 8 (over z, y), tensor: 2 (over core).
Axes of the slice: x: 2, y: 2, z: 4, core: 2. Of those that a mesh axis runs over, the one named last changes fastest.
Arguments:
- prompts: bfloat16 [48, 8192], P('groups'), parts along dimension 0, may hold values from -6 to 6
- gate_weight: bfloat16 [8192, 14848], P('pop', 'tensor'), may hold values from -0.0625 to 0.0625
- up_weight: bfloat16 [8192, 14848], P('pop', 'tensor'), may hold values from -0.0625 to 0.0625
- down_weight_matrix: bfloat16 [14848, 8192], P('tensor', 'pop'), may hold values from -0.046875 to 0.046875
- gate_in: bfloat16 [16, 8192, 4], P(('groups', 'pop')), parts along dimension 0, may hold values from -6 to 6
- gate_output_factors: bfloat16 [16, 14848, 4], P(('groups', 'pop'), 'tensor'), parts along dimension 0, may hold values from -6 to 6
- up_in: bfloat16 [16, 8192, 4], P(('groups', 'pop')), parts along dimension 0, may hold values from -6 to 6
- up_output_factors: bfloat16 [16, 14848, 4], P(('groups', 'pop'), 'tensor'), parts along dimension 0, may hold values from -6 to 6
- down_input_factors: bfloat16 [16, 14848, 4], P('groups', 'tensor'), parts along dimension 0, may hold values from -6 to 6
- down_out: bfloat16 [16, 8192, 4], P('groups', 'pop'), parts along dimension 0, may hold values from -6 to 6
- label_head: bfloat16 [8192, 128], P('tensor'), may hold values from -0.1875 to 0.1875
- targets: int32 [48], P('groups'), parts along dimension 0, may hold values from 0 to 127
Outputs:
- update: bfloat16 [29696, 8192], P(('groups', 'tensor'), 'pop'), parts along dimension 0
- scores: float32 [16], P(('groups', 'pop')), parts along dimension 0
There are 2 independent parts, one for each index of `groups`. A program takes and returns all parts, laid end to end along the dimension named above; an argument that names none is the same for every part. Nothing has to cross between parts.
All inputs are finite; a program needn't handle non-finite values.
Results may differ from a plain program's by a relative error of at most 0.023.
Values may be sent and summed in bfloat16 or wider, within the bound.
A program may use at most 256 MiB of HBM per device.

v0:
```python
import math
import jax
import jax.numpy as jnp
from jax import lax
from jax.sharding import PartitionSpec as P

noise_scale = 0.2
norm_eps = 1e-06


def scaled_rows(values):
    return values * lax.rsqrt(jnp.mean(values * values, axis=-1, keepdims=True) + norm_eps)


def build_hidden(
    gate_baseline, up_baseline, lowrank_gate, lowrank_up, gate_output_factors, up_output_factors
):
    gate_activation = gate_baseline.astype(jnp.float32)[None] + jnp.einsum(
        "hvw,hpw->hvp", lowrank_gate, gate_output_factors, preferred_element_type=jnp.float32
    )
    upper_bound = up_baseline.astype(jnp.float32)[None] + jnp.einsum(
        "hvw,hpw->hvp", lowrank_up, up_output_factors, preferred_element_type=jnp.float32
    )
    return (jax.nn.silu(gate_activation) * upper_bound).astype(jnp.bfloat16)


def label_terms(logits, targets):
    labels = logits.shape[1]
    picks = targets[:, None] == jnp.arange(labels, dtype=jnp.int32)[None, :]
    picked = jnp.sum(jnp.where(picks, logits, 0.0), axis=1)
    return picked - jnp.log(jnp.sum(jnp.exp(logits), axis=1))


def body(
    prompts,
    gate_weight,
    up_weight,
    down_weight_matrix,
    gate_in,
    gate_output_factors,
    up_in,
    up_output_factors,
    down_input_factors,
    down_out,
    label_head,
    targets,
):
    member = lax.axis_index("pop")
    width = prompts.shape[1]
    in_block = gate_weight.shape[0]
    ffn_half = gate_output_factors.shape[1]
    total_ff = ffn_half * lax.axis_size("tensor")
    members = down_input_factors.shape[0]
    rank = down_input_factors.shape[2]
    prompt_f = prompts.astype(jnp.float32)
    normed = scaled_rows(prompt_f).astype(jnp.bfloat16)
    own_cols = lax.dynamic_slice_in_dim(normed, member * in_block, in_block, 1)
    part_gate = jnp.dot(own_cols, gate_weight, preferred_element_type=jnp.float32)
    part_up = jnp.dot(own_cols, up_weight, preferred_element_type=jnp.float32)
    total_gate, total_up = lax.psum((part_gate, part_up), "pop")
    gate_baseline = total_gate.astype(jnp.bfloat16)
    up_baseline = total_up.astype(jnp.bfloat16)
    in_scale = noise_scale / math.sqrt(width)
    lowrank_gate = (
        in_scale * jnp.einsum("rd,mdk->mrk", normed, gate_in, preferred_element_type=jnp.float32)
    ).astype(jnp.bfloat16)
    lowrank_up = (
        in_scale * jnp.einsum("rd,mdk->mrk", normed, up_in, preferred_element_type=jnp.float32)
    ).astype(jnp.bfloat16)
    down_scale = noise_scale / math.sqrt(total_ff)
    hidden_state = build_hidden(
        gate_baseline, up_baseline, lowrank_gate, lowrank_up, gate_output_factors, up_output_factors
    )
    hidden_portion = lax.all_gather(hidden_state, "pop", axis=0, tiled=True)
    out_piece = down_out.astype(jnp.float32)
    entry_point = jnp.einsum(
        "uaz,zh->uah", hidden_portion, down_weight_matrix, preferred_element_type=jnp.float32
    )
    low_part = down_scale * jnp.einsum(
        "lpq,lqb->lpb", hidden_portion, down_input_factors, preferred_element_type=jnp.float32
    )
    partial_rows = entry_point + jnp.einsum(
        "mrk,mdk->mrd", low_part, out_piece, precision=lax.Precision.HIGHEST
    )
    rows_here = lax.all_to_all(partial_rows, "pop", split_axis=0, concat_axis=2, tiled=True)
    summed = lax.psum(rows_here, "tensor")[0]
    output = prompt_f + summed
    final = scaled_rows(output).astype(jnp.bfloat16)
    half = label_head.shape[0]
    own_half = lax.dynamic_slice_in_dim(final, lax.axis_index("tensor") * half, half, 1)
    logits = lax.psum(jnp.dot(own_half, label_head, preferred_element_type=jnp.float32), "tensor")
    reward = jnp.mean(label_terms(logits, targets))
    rewards = lax.all_gather(reward.reshape(1), "pop", axis=0, tiled=True)
    centre = jnp.mean(rewards)
    spread = jnp.mean((rewards - centre) * (rewards - centre))
    scores = (rewards - centre) * lax.rsqrt(spread + norm_eps)
    weighted = (scores[:, None, None] * down_out.astype(jnp.float32)).astype(jnp.bfloat16)
    update = jnp.einsum(
        "mfk,mdk->fd", down_input_factors, weighted, preferred_element_type=jnp.float32
    ) * (1.0 / math.sqrt(members * rank))
    own_score = lax.dynamic_slice_in_dim(scores, member, 1, 0)
    return (update.astype(jnp.bfloat16), own_score)


def solution(mesh):
    placed = (
        P("groups", None),
        P("pop", "tensor"),
        P("pop", "tensor"),
        P("tensor", "pop"),
        P(("groups", "pop"), None, None),
        P(("groups", "pop"), "tensor", None),
        P(("groups", "pop"), None, None),
        P(("groups", "pop"), "tensor", None),
        P("groups", "tensor", None),
        P("groups", "pop", None),
        P("tensor", None),
        P("groups"),
    )
    return jax.shard_map(
        body,
        mesh=mesh,
        in_specs=placed,
        out_specs=(P(("groups", "tensor"), "pop"), P(("groups", "pop"))),
        check_vma=False,
    )
```

profile of v0, /device:TPU:0, one launch (start us, length us, event | category | flops | bytes accessed | tf_op | source)
XLA Modules:
  0.0 282.1 jit_solution(8416717195286552256)
XLA Ops:
  7.2 1.3 fusion.8
  8.5 1.1 fusion.9
  9.7 7.6 %fusion.21 = f32[24,7424]{1,0:T(8,128)S(1)} fusion(bf16[1024,7424]{1,0:T(8,128)(2,1)} %param.14, bf16[24,8192]{1,0:T(8,128)(2,1)S(1)} %fusion.9, s32[]{:T(128)S(6)} %select_n.13), kind=kOutput, calls=%fused_computation.31 | convolution fusion | flops 364904448 | bytes 15966212 | tf_op jit(solution)/shard_map/dot_general | solution.py:59
  17.2 2.1 copy-done.2
  19.3 2.1 fusion.23
  21.4 80.8 %all-reduce.6 = (bf16[24,7424]{1,0:T(8,128)(2,1)S(1)}, bf16[24,7424]{1,0:T(8,128)(2,1)}) all-reduce(f32[24,7424]{1,0:T(8,128)S(1)} %fusion.23, f32[24,7424]{1,0:T(8,128)S(1)} %fusion.21), channel_id=1, replica_groups=mesh['groups'=2,'pop'=8,'tensor'=2] {'pop'}, use_global_device_ids=true, to_apply=%region_1.0 | all-reduce | flops 356352 | bytes 2138112 | tf_op jit(solution)/shard_map/psum | solution.py:60
  102.2 0.7 convolution_add_fusion.1
  102.9 2.4 fusion.5
  105.3 56.4 %all-gather.3.cloned.1.call-done = bf16[192,7424]{1,0:T(8,128)(2,1)} async-done(((bf16[24,7424]{1,0:T(8,128)(2,1)}), bf16[192,7424]{1,0:T(8,128)(2,1)}) %all-gather.3.cloned.1.call-update) | async-done | bytes 2850832 | tf_op jit(solution)/shard_map/all_gather | solution.py:74
  161.8 2.8 convolution_multiply_fusion
  164.6 7.9 %fusion.1 = f32[8,24,1024]{2,1,0:T(8,128)S(1)} fusion(bf16[8,24,7424]{2,1,0:T(8,128)(2,1)} %bitcast.50, bf16[7424,1024]{1,0:T(8,128)(2,1)} %param.15), kind=kOutput, calls=%fused_computation.2 | convolution fusion | flops 2919235584 | bytes 18841600 | tf_op jit(solution)/shard_map/uaz,zh->uah/dot_general | solution.py:76
  173.1 22.9 %all_to_all.18 = f32[8,24,1024]{2,1,0:T(8,128)S(1)} all-to-all(f32[8,24,1024]{2,1,0:T(8,128)S(1)} %convolution_add_fusion.2), channel_id=1, replica_groups=mesh['groups'=2,'pop'=8,'tensor'=2] {'pop'}, dimensions={0} | all-to-all | bytes 1572864 | tf_op jit(solution)/shard_map/all_to_all | solution.py:85
  196.0 0.9 copy.23
  197.0 0.6 dynamic-slice
  197.7 17.0 %all-reduce.5.cloned.1.call-done = f32[24,8192]{1,0:T(8,128)} async-done(((f32[24,8192]{1,0:T(8,128)}), f32[24,8192]{1,0:T(8,128)}) %all-reduce.5.cloned.1.call-update) | async-done | bytes 786448 | tf_op jit(solution)/shard_map/psum | solution.py:86
  214.6 1.4 multiply_reduce_fusion
  216.3 3.4 %psum.31 = f32[24,128]{1,0:T(8,128)S(1)} all-reduce(f32[24,128]{1,0:T(8,128)S(1)} %fusion.11), channel_id=1, replica_groups=mesh['groups'=2,'pop'=8,'tensor'=2] {'tensor'}, use_global_device_ids=true, to_apply=%region_5.6 | all-reduce | flops 3072 | bytes 24576 | tf_op jit(solution)/shard_map/psum | solution.py:91
  219.9 0.6 subtract_reduce_fusion
  221.2 0.7 dynamic-update-slice
  221.9 21.8 %all-reduce = f32[8]{0:T(128)S(1)} all-reduce(f32[8]{0:T(128)S(1)} %dynamic-update-slice), channel_id=1, replica_groups=mesh['groups'=2,'pop'=8,'tensor'=2] {'pop'}, use_global_device_ids=true, to_apply=%add | all-reduce | flops 8 | bytes 64
  243.7 0.6 reduce_sum.68
  245.0 0.6 multiply_reduce_fusion.1
  246.3 8.0 %fusion.3 = bf16[7424,1024]{0,1:T(8,128)(2,1)} fusion(bf16[8,7424,4]{1,2,0:T(4,128)(2,1)S(1)} %copy-done.8, bf16[8,1024,4]{1,2,0:T(4,128)(2,1)S(1)} %copy-done.5, f32[8]{0:T(128)S(1)} %subtract_multiply_fusion), kind=kOutput, calls=%fused_computation.4 | convolution fusion | flops 501841920 | bytes 15745056 | tf_op jit(solution)/shard_map/mfk,mdk->fd/dot_general | solution.py:98
  254.9 20.4 %copy.20 = bf16[7424,1024]{1,0:T(8,128)(2,1)} copy(bf16[7424,1024]{0,1:T(8,128)(2,1)} %fusion.3) | data formatting | bytes 30408704
  (35 shorter events, 1.8 us)
Async XLA Ops:
  7.2 208.8 %copy-start = (bf16[4096,128]{1,0:T(8,128)(2,1)S(1)}, bf16[4096,128]{1,0:T(8,128)(2,1)}, u32[]{:S(2)}) copy-start(bf16[4096,128]{1,0:T(8,128)(2,1)} %param.22) | copy-start | bytes 3145732
  7.2 154.6 %all-gather.3.cloned.1.call-start = ((), (), s32[]{:S(2)}) async-start(), calls=%async_computation.2 | async-start | bytes 3207168 | tf_op jit(solution)/shard_map/all_gather | solution.py:74
  9.6 9.7 %copy-start.2 = (bf16[1024,7424]{1,0:T(8,128)(2,1)S(1)}, bf16[1024,7424]{1,0:T(8,128)(2,1)}, u32[]{:S(2)}) copy-start(bf16[1024,7424]{1,0:T(8,128)(2,1)} %param.13) | copy-start | bytes 45613060
  19.3 82.9 %copy-start.4 = (bf16[1,8192,4]{1,2,0:T(4,128)(2,1)S(1)}, bf16[1,8192,4]{1,2,0:T(4,128)(2,1)}, u32[]{:S(2)}) copy-start(bf16[1,8192,4]{1,2,0:T(4,128)(2,1)} %param.16) | copy-start | bytes 196612
  19.3 82.9 %copy-start.6 = (bf16[1,7424,4]{1,2,0:T(4,128)(2,1)S(1)}, bf16[1,7424,4]{1,2,0:T(4,128)(2,1)}, u32[]{:S(2)}) copy-start(bf16[1,7424,4]{1,2,0:T(4,128)(2,1)} %param.17) | copy-start | bytes 178180
  19.3 83.5 %copy-start.9 = (bf16[1,8192,4]{1,2,0:T(4,128)(2,1)S(1)}, bf16[1,8192,4]{1,2,0:T(4,128)(2,1)}, u32[]{:S(2)}) copy-start(bf16[1,8192,4]{1,2,0:T(4,128)(2,1)} %param.18) | copy-start | bytes 196612
  19.3 83.6 %copy-start.10 = (bf16[1,7424,4]{1,2,0:T(4,128)(2,1)S(1)}, bf16[1,7424,4]{1,2,0:T(4,128)(2,1)}, u32[]{:S(2)}) copy-start(bf16[1,7424,4]{1,2,0:T(4,128)(2,1)} %param.19) | copy-start | bytes 178180
  105.3 109.4 %all-reduce.5.cloned.1.call-start = ((), (), s32[]{:S(2)}) async-start(), calls=%async_computation.1 | async-start | bytes 1572864 | tf_op jit(solution)/shard_map/psum | solution.py:86
  161.8 10.8 %copy-start.5 = (bf16[8,1024,4]{1,2,0:T(4,128)(2,1)S(1)}, bf16[8,1024,4]{1,2,0:T(4,128)(2,1)}, u32[]{:S(2)}) copy-start(bf16[8,1024,4]{1,2,0:T(4,128)(2,1)} %param.21) | copy-start | bytes 196612
  164.6 32.4 %copy-start.11 = (u32[32]{0:T(128)S(1)}, u32[32]{0:T(128)}, u32[]{:S(2)}) copy-start(u32[32]{0:T(128)} %constant.49) | copy-start | bytes 388
  164.6 50.1 %copy-start.3 = (bf16[24,8192]{1,0:T(8,128)(2,1)S(1)}, bf16[24,8192]{1,0:T(8,128)(2,1)}, u32[]{:S(2)}) copy-start(bf16[24,8192]{1,0:T(8,128)(2,1)} %param.12) | copy-start | bytes 1179652
  164.6 55.1 %copy-start.7 = (s32[24]{0:T(128)S(1)}, s32[24]{0:T(128)}, u32[]{:S(2)}) copy-start(s32[24]{0:T(128)} %param.23) | copy-start | bytes 292
  164.6 81.7 %copy-start.8 = (bf16[8,7424,4]{1,2,0:T(4,128)(2,1)S(1)}, bf16[8,7424,4]{1,2,0:T(4,128)(2,1)}, u32[]{:S(2)}) copy-start(bf16[8,7424,4]{1,2,0:T(4,128)(2,1)} %param.20) | copy-start | bytes 1425412
  254.3 21.0 %copy-start.1 = (bf16[4096,128]{1,0:T(8,128)(2,1)S(1)}, bf16[4096,128]{1,0:T(8,128)(2,1)}, u32[]{:S(2)}) copy-start(bf16[4096,128]{1,0:T(8,128)(2,1)} %param.22) | copy-start | bytes 3145732
Sparse Core Ops, SparseCore 0:
  105.4 56.3 all-gather.2
  197.1 17.4 all-reduce.4
where the time goes:
time: 283 us; the launch traced here: 282 us
  blocking collectives  129 us (46%)
  waiting for transfers between devices  73.5 us (26%)
  matrix products  32.3 us (11%)
  local copies, waits for them, and re-layouts  25.4 us (9%)
  between operations  16.2 us (6%)
  other arithmetic  5.78 us (2%)
    psum x1, blocking collectives, body(): total_gate, total_up = lax.psum((part_gate, part_up), 'pop')  80.8 us
    all_gather x1, waiting for transfers between devices, body(): hidden_portion = lax.all_gather(hidden_state, 'pop', axis=0, tiled=True)  56.4 us
    unnamed x29, local copies, waits for them, and re-layouts  24.8 us
    all_to_all x1, blocking collectives, body(): lax.all_to_all(partial_rows, 'pop', split_axis=0, concat_axis=2, tiled=True)  22.9 us
    unnamed x1, blocking collectives  21.8 us
    psum x1, waiting for transfers between devices, body(): summed = lax.psum(rows_here, 'tensor')[0]  17 us
    dot_general x1, matrix products, body(): jnp.einsum('mfk,mdk->fd', down_input_factors, weighted, preferred_element...  7.97 us
    dot_general x1, matrix products, body(): jnp.einsum('uaz,zh->uah', hidden_portion, down_weight_matrix, preferred_e...  7.93 us
  transfers between devices with their start and end apart: 2, of which 2 were waited for; matrix products, arithmetic and copies ran while one was open for 0% of the time, Pallas kernels for 0%

commit v1 on v0

--- a/solution.py
+++ b/solution.py
@@ -71,7 +71,15 @@
     hidden_state = build_hidden(
         gate_baseline, up_baseline, lowrank_gate, lowrank_up, gate_output_factors, up_output_factors
     )
-    hidden_portion = lax.all_gather(hidden_state, "pop", axis=0, tiled=True)
+    ways, here = (lax.axis_size("pop"), lax.axis_index("pop"))
+    grown, reach = (hidden_state, 1)
+    while reach < ways:
+        theirs = lax.ppermute(grown, "pop", [(d, d ^ reach) for d in range(ways)])
+        mine_first = jnp.concatenate([grown, theirs], axis=0)
+        theirs_first = jnp.concatenate([theirs, grown], axis=0)
+        grown = jnp.where(here & reach == 0, mine_first, theirs_first)
+        reach = 2 * reach
+    hidden_portion = grown
     out_piece = down_out.astype(jnp.float32)
     entry_point = jnp.einsum(
         "uaz,zh->uah", hidden_portion, down_weight_matrix, preferred_element_type=jnp.float32

time: 283 us -> 299 us (1.057)
  waiting for transfers between devices: 73.5 us -> 88.5 us
  blocking collectives: 129 us -> 125 us
    ppermute x0 -> x3, waiting for transfers between devices: none -> 71 us  [body(): theirs = lax.ppermute(grown, 'pop', [(d, d ^ reach) for d in range(ways)])]
    all_gather x1 -> x0, waiting for transfers between devices: 56.4 us -> none  [body(): hidden_portion = lax.all_gather(hidden_state, 'pop', axis=0, tiled=True)]
    all_to_all x1, blocking collectives: 22.9 us -> 18.6 us  [body(): lax.all_to_all(partial_rows, 'pop', split_axis=0, concat_axis=2, tiled=True)]
    unnamed x29 -> x25, local copies, waits for them, and re-layouts: 24.8 us -> 24.9 us
  transfers between devices with their start and end apart: 2 -> 4, of which waited for: 2 -> 4; matrix products, arithmetic and copies ran while one was open for 0% -> 0% of each run, Pallas kernels for 0% -> 0%
where the time goes in v1:
time: 299 us; the launch traced here: 298 us
  blocking collectives  125 us (42%)
  waiting for transfers between devices  88.5 us (30%)
  matrix products  33.2 us (11%)
  local copies, waits for them, and re-layouts  25.5 us (9%)
  between operations  16.2 us (5%)
  other arithmetic  7.41 us (2%)
    psum x1, blocking collectives, body(): total_gate, total_up = lax.psum((part_gate, part_up), 'pop')  80.9 us
    ppermute x3, waiting for transfers between devices, body(): theirs = lax.ppermute(grown, 'pop', [(d, d ^ reach) for d in range(ways)])  71 us
    unnamed x25, local copies, waits for them, and re-layouts  24.9 us
    unnamed x1, blocking collectives  21.8 us
    all_to_all x1, blocking collectives, body(): lax.all_to_all(partial_rows, 'pop', split_axis=0, concat_axis=2, tiled=True)  18.6 us
    psum x1, waiting for transfers between devices, body(): summed = lax.psum(rows_here, 'tensor')[0]  17.4 us
    dot_general x1, matrix products, body(): jnp.einsum('uaz,zh->uah', hidden_portion, down_weight_matrix, preferred_e...  9.37 us
    dot_general x1, matrix products, body(): jnp.einsum('mfk,mdk->fd', down_input_factors, weighted, preferred_element...  7.96 us
  transfers between devices with their start and end apart: 4, of which 4 were waited for; matrix products, arithmetic and copies ran while one was open for 0% of the time, Pallas kernels for 0%

profile of v1, /device:TPU:0, one launch (start us, length us, event | category | flops | bytes accessed | tf_op | source)
XLA Modules:
  0.0 297.7 jit_solution(7578767713857571869)
XLA Ops:
  7.2 1.3 fusion.12
  8.5 1.1 fusion.13
  9.7 7.6 %fusion.25 = f32[24,7424]{1,0:T(8,128)S(1)} fusion(bf16[1024,7424]{1,0:T(8,128)(2,1)} %param.14, bf16[24,8192]{1,0:T(8,128)(2,1)S(1)} %fusion.13, s32[]{:T(128)S(6)} %select_n.40), kind=kOutput, calls=%fused_computation.35 | convolution fusion | flops 364904448 | bytes 15966212 | tf_op jit(solution)/shard_map/dot_general | solution.py:59
  17.2 2.1 copy-done.2
  19.3 2.1 fusion.27
  21.4 80.9 %all-reduce.6 = (bf16[24,7424]{1,0:T(8,128)(2,1)S(1)}, bf16[24,7424]{1,0:T(8,128)(2,1)}) all-reduce(f32[24,7424]{1,0:T(8,128)S(1)} %fusion.27, f32[24,7424]{1,0:T(8,128)S(1)} %fusion.25), channel_id=1, replica_groups=mesh['groups'=2,'pop'=8,'tensor'=2] {'pop'}, use_global_device_ids=true, to_apply=%region_1.0 | all-reduce | flops 356352 | bytes 2138112 | tf_op jit(solution)/shard_map/psum | solution.py:60
  103.0 1.7 fusion.6
  104.7 1.0 collective-permute-start
  105.7 6.4 %collective-permute-done = bf16[1,24,7424]{2,1,0:T(8,128)(2,1)S(1)} collective-permute-done((bf16[1,24,7424]{2,1,0:T(8,128)(2,1)S(1)}, bf16[1,24,7424]{2,1,0:T(8,128)(2,1)S(1)}, u32[]{:S(2)}, u32[]{:S(2)}) %collective-permute-start) | collective-permute-done | bytes 356384 | tf_op jit(solution)/shard_map/ppermute | solution.py:77
  112.3 16.0 %collective-permute-done.1 = bf16[2,24,7424]{2,1,0:T(8,128)(2,1)} collective-permute-done((bf16[2,24,7424]{2,1,0:T(8,128)(2,1)S(1)}, bf16[2,24,7424]{2,1,0:T(8,128)(2,1)}, u32[]{:S(2)}, u32[]{:S(2)}) %collective-permute-start.1) | collective-permute-done | bytes 712736 | tf_op jit(solution)/shard_map/ppermute | solution.py:77
  128.3 1.5 maximum_select_fusion.1
  129.9 1.1 collective-permute-start.2
  131.0 48.6 %collective-permute-done.2 = bf16[4,24,7424]{2,1,0:T(8,128)(2,1)} collective-permute-done((bf16[4,24,7424]{2,1,0:T(8,128)(2,1)S(1)}, bf16[4,24,7424]{2,1,0:T(8,128)(2,1)}, u32[]{:S(2)}, u32[]{:S(2)}) %collective-permute-start.2) | collective-permute-done | bytes 1425440 | tf_op jit(solution)/shard_map/ppermute | solution.py:77
  179.6 3.0 convolution_multiply_fusion
  183.1 9.4 %fusion.7 = f32[8,24,1024]{2,1,0:T(8,128)S(1)} fusion(f32[8,24,1024]{2,1,0:T(8,128)S(1)} %fusion.38, bf16[7424,1024]{1,0:T(8,128)(2,1)} %param.15, bf16[4,24,7424]{2,1,0:T(8,128)(2,1)} %collective-permute-done.2, bf16[4,24,7424]{2,1,0:T(8,128)(2,1)S(1)} %maximum_select_fusion.1, pred[]{:T(512)S(6)} %eq.25), kind=kOutput, calls=%fused_computation.12 | convolution fusion | flops 2923708416 | bytes 19628032 | tf_op jit(solution)/shard_map/uaz,zh->uah/dot_general | solution.py:84
  192.6 18.6 %all_to_all.18 = f32[8,24,1024]{2,1,0:T(8,128)S(1)} all-to-all(f32[8,24,1024]{2,1,0:T(8,128)S(1)} %fusion.7), channel_id=1, replica_groups=mesh['groups'=2,'pop'=8,'tensor'=2] {'pop'}, dimensions={0} | all-to-all | bytes 1572864 | tf_op jit(solution)/shard_map/all_to_all | solution.py:93
  211.1 0.9 copy.23
  212.7 17.4 %all-reduce.5.cloned.1.call-done = f32[24,8192]{1,0:T(8,128)} async-done(((f32[24,8192]{1,0:T(8,128)}), f32[24,8192]{1,0:T(8,128)}) %all-reduce.5.cloned.1.call-update) | async-done | bytes 786448 | tf_op jit(solution)/shard_map/psum | solution.py:94
  230.2 1.3 multiply_reduce_fusion
  231.9 3.4 %psum.31 = f32[24,128]{1,0:T(8,128)S(1)} all-reduce(f32[24,128]{1,0:T(8,128)S(1)} %fusion.15), channel_id=1, replica_groups=mesh['groups'=2,'pop'=8,'tensor'=2] {'tensor'}, use_global_device_ids=true, to_apply=%region_5.6 | all-reduce | flops 3072 | bytes 24576 | tf_op jit(solution)/shard_map/psum | solution.py:99
  236.7 0.7 dynamic-update-slice
  237.4 21.8 %all-reduce = f32[8]{0:T(128)S(1)} all-reduce(f32[8]{0:T(128)S(1)} %dynamic-update-slice), channel_id=1, replica_groups=mesh['groups'=2,'pop'=8,'tensor'=2] {'pop'}, use_global_device_ids=true, to_apply=%add | all-reduce | flops 8 | bytes 64
  261.8 8.0 %fusion.3 = bf16[7424,1024]{0,1:T(8,128)(2,1)} fusion(bf16[8,7424,4]{1,2,0:T(4,128)(2,1)S(1)} %copy-done.8, bf16[8,1024,4]{1,2,0:T(4,128)(2,1)S(1)} %copy-done.5, f32[8]{0:T(128)S(1)} %subtract_multiply_fusion), kind=kOutput, calls=%fused_computation.4 | convolution fusion | flops 501841920 | bytes 15745056 | tf_op jit(solution)/shard_map/mfk,mdk->fd/dot_general | solution.py:106
  270.4 20.5 %copy.20 = bf16[7424,1024]{1,0:T(8,128)(2,1)} copy(bf16[7424,1024]{0,1:T(8,128)(2,1)} %fusion.3) | data formatting | bytes 30408704
  (36 shorter events, 5.1 us)
Async XLA Ops:
  7.2 224.4 %copy-start = (bf16[4096,128]{1,0:T(8,128)(2,1)S(1)}, bf16[4096,128]{1,0:T(8,128)(2,1)}, u32[]{:S(2)}) copy-start(bf16[4096,128]{1,0:T(8,128)(2,1)} %param.22) | copy-start | bytes 3145732
  7.2 223.0 %all-reduce.5.cloned.1.call-start = ((), (), s32[]{:S(2)}) async-start(), calls=%async_computation.1 | async-start | bytes 1572864 | tf_op jit(solution)/shard_map/psum | solution.py:94
  9.6 9.7 %copy-start.2 = (bf16[1024,7424]{1,0:T(8,128)(2,1)S(1)}, bf16[1024,7424]{1,0:T(8,128)(2,1)}, u32[]{:S(2)}) copy-start(bf16[1024,7424]{1,0:T(8,128)(2,1)} %param.13) | copy-start | bytes 45613060
  19.3 83.0 %copy-start.4 = (bf16[1,8192,4]{1,2,0:T(4,128)(2,1)S(1)}, bf16[1,8192,4]{1,2,0:T(4,128)(2,1)}, u32[]{:S(2)}) copy-start(bf16[1,8192,4]{1,2,0:T(4,128)(2,1)} %param.16) | copy-start | bytes 196612
  19.3 83.0 %copy-start.6 = (bf16[1,7424,4]{1,2,0:T(4,128)(2,1)S(1)}, bf16[1,7424,4]{1,2,0:T(4,128)(2,1)}, u32[]{:S(2)}) copy-start(bf16[1,7424,4]{1,2,0:T(4,128)(2,1)} %param.17) | copy-start | bytes 178180
  104.7 7.4 %collective-permute-start = (bf16[1,24,7424]{2,1,0:T(8,128)(2,1)S(1)}, bf16[1,24,7424]{2,1,0:T(8,128)(2,1)S(1)}, u32[]{:S(2)}, u32[]{:S(2)}) collective-permute-start(bf16[1,24,7424]{2,1,0:T(8,128)(2,1)S(1)} %fusion.6), channel_id=1, source_target_pairs={{0,2},{2,0},{4,6},{6,4},{8,10},{10,8},{12,14},{14,12},{1,3},{3,1},... | collective-permute-start | bytes 1069064 | tf_op jit(solution)/shard_map/ppermute | solution.py:77
  112.3 16.1 %collective-permute-start.1 = (bf16[2,24,7424]{2,1,0:T(8,128)(2,1)S(1)}, bf16[2,24,7424]{2,1,0:T(8,128)(2,1)}, u32[]{:S(2)}, u32[]{:S(2)}) collective-permute-start(bf16[2,24,7424]{2,1,0:T(8,128)(2,1)S(1)} %maximum_select_fusion.2), channel_id=1, source_target_pairs={{0,4},{2,6},{4,0},{6,2},{8,12},{10,14},{12,8},{14,10},{1,5},{3,7},... | collective-permute-start | bytes 2138120 | tf_op jit(solution)/shard_map/ppermute | solution.py:77
  129.9 49.7 %collective-permute-start.2 = (bf16[4,24,7424]{2,1,0:T(8,128)(2,1)S(1)}, bf16[4,24,7424]{2,1,0:T(8,128)(2,1)}, u32[]{:S(2)}, u32[]{:S(2)}) collective-permute-start(bf16[4,24,7424]{2,1,0:T(8,128)(2,1)S(1)} %maximum_select_fusion.1), channel_id=1, source_target_pairs={{0,8},{2,10},{4,12},{6,14},{8,0},{10,2},{12,4},{14,6},{1,9},{3,11}... | collective-permute-start | bytes 4276232 | tf_op jit(solution)/shard_map/ppermute | solution.py:77
  131.0 51.6 %copy-start.5 = (bf16[8,1024,4]{1,2,0:T(4,128)(2,1)S(1)}, bf16[8,1024,4]{1,2,0:T(4,128)(2,1)}, u32[]{:S(2)}) copy-start(bf16[8,1024,4]{1,2,0:T(4,128)(2,1)} %param.21) | copy-start | bytes 196612
  192.5 19.6 %copy-start.9 = (u32[32]{0:T(128)S(1)}, u32[32]{0:T(128)}, u32[]{:S(2)}) copy-start(u32[32]{0:T(128)} %constant.55) | copy-start | bytes 388
  192.5 37.7 %copy-start.3 = (bf16[24,8192]{1,0:T(8,128)(2,1)S(1)}, bf16[24,8192]{1,0:T(8,128)(2,1)}, u32[]{:S(2)}) copy-start(bf16[24,8192]{1,0:T(8,128)(2,1)} %param.12) | copy-start | bytes 1179652
  211.1 24.1 %copy-start.7 = (s32[24]{0:T(128)S(1)}, s32[24]{0:T(128)}, u32[]{:S(2)}) copy-start(s32[24]{0:T(128)} %param.23) | copy-start | bytes 292
  211.1 50.7 %copy-start.8 = (bf16[8,7424,4]{1,2,0:T(4,128)(2,1)S(1)}, bf16[8,7424,4]{1,2,0:T(4,128)(2,1)}, u32[]{:S(2)}) copy-start(bf16[8,7424,4]{1,2,0:T(4,128)(2,1)} %param.20) | copy-start | bytes 1425412
  270.4 20.5 %copy-start.1 = (bf16[4096,128]{1,0:T(8,128)(2,1)S(1)}, bf16[4096,128]{1,0:T(8,128)(2,1)}, u32[]{:S(2)}) copy-start(bf16[4096,128]{1,0:T(8,128)(2,1)} %param.22) | copy-start | bytes 3145732
Sparse Core Ops, SparseCore 0:
  212.2 17.9 all-reduce.4
